TPU v7x, 256 devices: a whole 4x4x8 slice. The times are simulated.
256 devices in a mesh: seq: 32 (over y, z), mp: 8 (over x, core).
Axes of the slice: x: 4, y: 4, z: 8, core: 2. Of those that a mesh axis runs over, the one named last changes fastest.
Arguments:
- out_grad: bfloat16 [16384, 8192], P('seq', 'mp'), may hold values from -6 to 6
- out_weight: bfloat16 [4096, 8192], P('mp'), may hold values from -0.0625 to 0.0625
- queries: bfloat16 [16384, 4096], P('seq', 'mp'), may hold values from -5 to 5
- keys: bfloat16 [64, 128, 4096], P('seq', None, 'mp'), may hold values from -5 to 5
- values: bfloat16 [64, 128, 4096], P('seq', None, 'mp'), may hold values from -6 to 6
- retrieval: int32 [256, 2], replicated, may hold values from 0 to 63, as said below
- counts: int32 [256], P('seq'), may hold values from 1 to 2
Outputs:
- query_grad: bfloat16 [16384, 4096], P('seq', 'mp')
- key_grad: bfloat16 [64, 128, 4096], P('seq', None, 'mp')
- value_grad: bfloat16 [64, 128, 4096], P('seq', None, 'mp')
Inputs may be any that keep to these rules, and one draw needn't show every extreme that they name: `retrieval`: entry e is held by index e // 2 of seq. The 16 neighbour places of one index's blocks name entries of any one owner at most 1 times, and some owner is named exactly 1 times by the blocks of every index.
All inputs are finite; a program needn't handle non-finite values.
Results may differ from a plain program's by a relative error of at most 0.0091.
Values may be sent and summed in bfloat16 or wider, within the bound.
A program may use at most 128 MiB of HBM per device.

v0:
```python
import math
import jax
import jax.numpy as jnp
from jax import lax
from jax.sharding import PartitionSpec as P

HEAD = 128
BLOCK = 64
NEIGH = 2


def rank_slots(owners):
    slot_total = owners.shape[-1]
    earlier_mask = jnp.arange(slot_total)[None, :] < jnp.arange(slot_total)[:, None]
    same_owner = owners[..., :, None] == owners[..., None, :]
    return jnp.sum(same_owner & earlier_mask, axis=-1)


def on_device(out_grad, out_weight, queries, keys, values, retrieval, counts):
    seq_count = lax.axis_size("seq")
    my_index = lax.axis_index("seq")
    tok_rows, head_cols = queries.shape
    entries_here = keys.shape[0]
    nbr_rows = keys.shape[1]
    heads_here = head_cols // HEAD
    blocks_here = tok_rows // BLOCK
    slot_count = blocks_here * NEIGH
    slot_cap = (slot_count + seq_count - 1) // seq_count
    score_scale = 1.0 / math.sqrt(HEAD)
    grad_out = lax.dot_general(
        lax.all_gather(out_grad, "mp", axis=1, tiled=True),
        out_weight,
        (((1,), (1,)), ((), ())),
        preferred_element_type=jnp.float32,
    ).astype(jnp.bfloat16)
    all_lists = retrieval.reshape(seq_count, slot_count)
    owners = all_lists // entries_here
    all_ranks = rank_slots(owners)
    my_lists = lax.dynamic_index_in_dim(all_lists, my_index, 0, keepdims=False)
    my_owner = my_lists // entries_here
    my_rank = lax.dynamic_index_in_dim(all_ranks, my_index, 0, keepdims=False)
    flat_slot = my_owner * slot_cap + my_rank
    chosen = (owners == my_index)[:, None, :] & (
        all_ranks[:, None, :] == jnp.arange(slot_cap)[None, :, None]
    )
    filled = jnp.any(chosen, axis=2)
    picked = jnp.sum(jnp.where(chosen, all_lists[:, None, :] % entries_here, 0), axis=2)
    all_keys, all_values = (
        lax.all_gather(keys, "seq", axis=0, tiled=True),
        lax.all_gather(values, "seq", axis=0, tiled=True),
    )
    slot_keys = jnp.take(all_keys, my_lists, axis=0)
    slot_values = jnp.take(all_values, my_lists, axis=0)
    query_rows = queries.reshape(blocks_here, BLOCK, heads_here, HEAD)
    grad_rows = grad_out.reshape(blocks_here, BLOCK, heads_here, HEAD)
    key_rows = slot_keys.reshape(blocks_here, NEIGH * nbr_rows, heads_here, HEAD)
    value_rows = slot_values.reshape(blocks_here, NEIGH * nbr_rows, heads_here, HEAD)
    live_keys = jnp.arange(NEIGH * nbr_rows)[None, :] < (counts * nbr_rows)[:, None]
    live_mask = live_keys[:, None, None, :]
    scores = (
        jnp.einsum("cqhe,ckhe->chqk", query_rows, key_rows, preferred_element_type=jnp.float32)
        * score_scale
    )
    row_max = jnp.max(jnp.where(live_mask, scores, -jnp.inf), axis=-1, keepdims=True)
    raised = jnp.where(live_mask, jnp.exp(scores - row_max), 0.0)
    attn_weights = raised / jnp.sum(raised, axis=-1, keepdims=True)
    weights_low = attn_weights.astype(jnp.bfloat16)
    attn_out = jnp.einsum(
        "chqk,ckhe->cqhe", weights_low, value_rows, preferred_element_type=jnp.float32
    )
    row_dot = jnp.sum(grad_rows.astype(jnp.float32) * attn_out, axis=-1)
    grad_weights = jnp.einsum(
        "cqhe,ckhe->chqk", grad_rows, value_rows, preferred_element_type=jnp.float32
    )
    grad_scores = attn_weights * (grad_weights - jnp.transpose(row_dot, (0, 2, 1))[..., None])
    grad_low = grad_scores.astype(jnp.bfloat16)
    query_grad = (
        (
            jnp.einsum("chqk,ckhe->cqhe", grad_low, key_rows, preferred_element_type=jnp.float32)
            * score_scale
        )
        .astype(jnp.bfloat16)
        .reshape(tok_rows, head_cols)
    )
    key_terms = (
        (
            jnp.einsum("chqk,cqhe->ckhe", grad_low, query_rows, preferred_element_type=jnp.float32)
            * score_scale
        )
        .astype(jnp.bfloat16)
        .reshape(slot_count, nbr_rows, head_cols)
    )
    value_terms = (
        jnp.einsum("chqk,cqhe->ckhe", weights_low, grad_rows, preferred_element_type=jnp.float32)
        .astype(jnp.bfloat16)
        .reshape(slot_count, nbr_rows, head_cols)
    )
    key_back = (
        jnp.zeros((seq_count * slot_cap, nbr_rows, head_cols), jnp.bfloat16)
        .at[flat_slot]
        .set(key_terms)
        .reshape(seq_count, slot_cap, nbr_rows, head_cols)
    )
    value_back = (
        jnp.zeros((seq_count * slot_cap, nbr_rows, head_cols), jnp.bfloat16)
        .at[flat_slot]
        .set(value_terms)
        .reshape(seq_count, slot_cap, nbr_rows, head_cols)
    )
    back_keys, back_values = (
        lax.all_to_all(key_back, "seq", split_axis=0, concat_axis=0, tiled=True),
        lax.all_to_all(value_back, "seq", split_axis=0, concat_axis=0, tiled=True),
    )
    summing = (
        ((picked[None, :, :] == jnp.arange(entries_here)[:, None, None]) & filled[None, :, :])
        .astype(jnp.bfloat16)
        .reshape(entries_here, seq_count * slot_cap)
    )
    key_grad = (
        jnp.dot(
            summing,
            back_keys.reshape(seq_count * slot_cap, nbr_rows * head_cols),
            preferred_element_type=jnp.float32,
        )
        .astype(jnp.bfloat16)
        .reshape(entries_here, nbr_rows, head_cols)
    )
    value_grad = (
        jnp.dot(
            summing,
            back_values.reshape(seq_count * slot_cap, nbr_rows * head_cols),
            preferred_element_type=jnp.float32,
        )
        .astype(jnp.bfloat16)
        .reshape(entries_here, nbr_rows, head_cols)
    )
    return (query_grad, key_grad, value_grad)


def solution(mesh):
    return jax.shard_map(
        on_device,
        mesh=mesh,
        in_specs=(
            P("seq", "mp"),
            P("mp", None),
            P("seq", "mp"),
            P("seq", None, "mp"),
            P("seq", None, "mp"),
            P(),
            P("seq"),
        ),
        out_specs=(P("seq", "mp"), P("seq", None, "mp"), P("seq", None, "mp")),
        check_vma=False,
    )
```

profile of v0, /device:TPU:2, one launch (start us, length us, event | category | flops | bytes accessed | tf_op | source)
XLA Modules:
  0.0 513.0 jit_solution(1532240102834940952)
XLA Ops:
  7.2 0.7 all-gather.6.cloned.1.call-update
  8.0 0.7 all-gather.4.cloned.1.call-update
  8.7 0.7 all-gather.8.cloned.1.call-update
  9.4 0.8 copy.93
  10.2 0.1 reshape.442
  10.3 0.1 reshape.444
  10.6 0.1 convert_reduce_fusion
  10.7 0.2 dynamic-slice_reduce_fusion
  11.0 53.3 %all-gather.6.cloned.1.call-done = bf16[512,8192]{1,0:T(8,128)(2,1)} async-done(((bf16[512,1024]{1,0:T(8,128)(2,1)}), bf16[512,8192]{1,0:T(8,128)(2,1)}) %all-gather.6.cloned.1.call-update) | async-done | bytes 8388624 | tf_op jit(solution)/shard_map/all_gather | solution.py:31
  64.3 10.3 %convolution_convert_fusion.2 = bf16[512,512]{1,0:T(8,128)(2,1)S(1)} fusion(bf16[512,8192]{1,0:T(8,128)(2,1)} %all-gather.6.cloned.1.call-done, bf16[512,8192]{1,0:T(8,128)(2,1)} %param.10), kind=kOutput, calls=%fused_computation.31 | convolution fusion | flops 4295229440 | bytes 17301504 | tf_op jit(solution)/shard_map/dot_general | solution.py:30
  74.6 0.1 reshape.445
  74.7 91.7 %all-gather.4.cloned.1.call-done = bf16[64,128,512]{2,1,0:T(8,128)(2,1)} async-done(((bf16[2,128,512]{2,1,0:T(8,128)(2,1)}), bf16[64,128,512]{2,1,0:T(8,128)(2,1)}) %all-gather.4.cloned.1.call-update) | async-done | bytes 8388624 | tf_op jit(solution)/shard_map/all_gather | solution.py:49
  166.4 4.1 gather_fusion
  170.5 94.1 %all-gather.8.cloned.1.call-done = bf16[64,128,512]{2,1,0:T(8,128)(2,1)} async-done(((bf16[2,128,512]{2,1,0:T(8,128)(2,1)}), bf16[64,128,512]{2,1,0:T(8,128)(2,1)}) %all-gather.8.cloned.1.call-update) | async-done | bytes 8388624 | tf_op jit(solution)/shard_map/all_gather | solution.py:50
  264.7 5.4 %gather_fusion.1 = bf16[16,128,512]{2,1,0:T(8,128)(2,1)} fusion(bf16[64,128,512]{2,1,0:T(8,128)(2,1)} %all-gather.8.cloned.1.call-done, s32[1024]{0:T(1024)S(1)} %pad_clamp_fusion), kind=kCustom, calls=%fused_computation.1.clone | custom fusion | bytes 4194368 | tf_op jit(solution)/shard_map/jit(_take)/gather | solution.py:53
  270.1 4.0 broadcast_select_fusion.1
  274.0 2.5 reshape.443
  276.6 0.8 fusion.5
  277.4 0.5 copy-done.1
  277.9 1.7 bitcast_reduce_fusion
  279.7 1.3 copy-done.8
  281.0 0.9 convert_bitcast_fusion
  281.9 2.5 copy.120
  284.4 2.7 reshape.496
  287.1 2.4 broadcast.352.clone
  289.6 5.2 %scatter_fusion.1 = bf16[32,128,512]{2,1,0:T(8,128)(2,1)} fusion(bf16[32,128,512]{2,1,0:T(8,128)(2,1)} %broadcast.352.clone, s32[16]{0:T(128)S(1)} %fusion.53, bf16[16,128,512]{2,1,0:T(8,128)(2,1)S(1)} %reshape.496), kind=kCustom, calls=%fused_computation.3 | custom fusion | bytes 6291520 | tf_op jit(solution)/shard_map/scatter | solution.py:107
  294.8 6.1 %all-to-all-start.1 = ((bf16[32,1,128,512]{3,2,1,0:T(8,128)(2,1)}), bf16[32,1,128,512]{3,2,1,0:T(8,128)(2,1)}, u32[]{:S(2)}, u32[]{:S(2)}) async-start(bf16[32,1,128,512]{3,2,1,0:T(8,128)(2,1)} %bitcast.79), calls=%async_computation.1 | async-start | bytes 8388608 | tf_op jit(solution)/shard_map/all_to_all | solution.py:112
  300.9 2.1 reshape.446
  302.9 3.1 fusion.28
  306.0 0.4 copy-done.9
  306.4 1.0 multiply_convert_fusion.1
  307.5 0.8 fusion.13
  308.3 0.1 copy-done.5
  308.4 2.9 copy.119
  311.4 2.7 reshape.495
  314.1 2.4 broadcast.352.clone.1
  316.5 5.2 %scatter_fusion = bf16[32,128,512]{2,1,0:T(8,128)(2,1)} fusion(bf16[32,128,512]{2,1,0:T(8,128)(2,1)} %broadcast.352.clone.1, s32[16]{0:T(128)S(1)} %fusion.53, bf16[16,128,512]{2,1,0:T(8,128)(2,1)S(1)} %reshape.495), kind=kCustom, calls=%fused_computation.2 | custom fusion | bytes 6291520 | tf_op jit(solution)/shard_map/scatter | solution.py:101
  321.8 75.5 %all-to-all-done.1 = bf16[32,1,128,512]{3,2,1,0:T(8,128)(2,1)} async-done(((bf16[32,1,128,512]{3,2,1,0:T(8,128)(2,1)}), bf16[32,1,128,512]{3,2,1,0:T(8,128)(2,1)}, u32[]{:S(2)}, u32[]{:S(2)}) %all-to-all-start.1) | async-done | bytes 4194336 | tf_op jit(solution)/shard_map/all_to_all | solution.py:112
  397.3 5.5 %all-to-all-start = ((bf16[32,1,128,512]{3,2,1,0:T(8,128)(2,1)}), bf16[32,1,128,512]{3,2,1,0:T(8,128)(2,1)}, u32[]{:S(2)}, u32[]{:S(2)}) async-start(bf16[32,1,128,512]{3,2,1,0:T(8,128)(2,1)} %bitcast.78), calls=%async_computation | async-start | bytes 8388608 | tf_op jit(solution)/shard_map/all_to_all | solution.py:111
  403.1 1.7 fusion.31
  404.7 0.4 copy.101
  405.2 0.9 copy.162
  406.0 6.5 %copy.126 = bf16[4,8,128,512]{3,1,2,0:T(8,128)(2,1)} copy(bf16[4,8,128,512]{3,2,1,0:T(8,128)(2,1)} %bitcast.27) | data formatting | bytes 8388608
  412.5 87.0 %all-to-all-done = bf16[32,1,128,512]{3,2,1,0:T(8,128)(2,1)} async-done(((bf16[32,1,128,512]{3,2,1,0:T(8,128)(2,1)}), bf16[32,1,128,512]{3,2,1,0:T(8,128)(2,1)}, u32[]{:S(2)}, u32[]{:S(2)}) %all-to-all-start) | async-done | bytes 4194336 | tf_op jit(solution)/shard_map/all_to_all | solution.py:111
  499.6 4.7 copy.124
  504.3 0.7 convolution_convert_fusion
  504.9 0.7 convolution_convert_fusion.1
  505.6 0.8 copy_bitcast_fusion.1
  (31 shorter events, 0.6 us)
Async XLA Ops:
  7.2 3.2 copy-start.6
  7.2 3.7 copy-start.7
  7.2 57.1 %all-gather.6.cloned.1.call-start = ((), (), s32[]{:S(2)}) async-start(), calls=%async_computation.3 | async-start | bytes 9437184 | tf_op jit(solution)/shard_map/all_gather | solution.py:31
  7.9 158.5 %all-gather.4.cloned.1.call-start = ((), (), s32[]{:S(2)}) async-start(), calls=%async_computation.2 | async-start | bytes 8650752 | tf_op jit(solution)/shard_map/all_gather | solution.py:49
  8.7 256.0 %all-gather.8.cloned.1.call-start = ((), (), s32[]{:S(2)}) async-start(), calls=%async_computation.4 | async-start | bytes 8650752 | tf_op jit(solution)/shard_map/all_gather | solution.py:50
  276.6 1.4 copy-start.1
  279.7 1.3 copy-start.8
  294.8 6.1 %copy-start.3 = (bf16[16,128,512]{2,1,0:T(8,128)(2,1)S(1)}, bf16[16,128,512]{2,1,0:T(8,128)(2,1)}, u32[]{:S(2)}) copy-start(bf16[16,128,512]{2,1,0:T(8,128)(2,1)} %get-tuple-element.9) | copy-start | bytes 6291460
  294.8 102.5 %all-to-all-start.1 = ((bf16[32,1,128,512]{3,2,1,0:T(8,128)(2,1)}), bf16[32,1,128,512]{3,2,1,0:T(8,128)(2,1)}, u32[]{:S(2)}, u32[]{:S(2)}) async-start(bf16[32,1,128,512]{3,2,1,0:T(8,128)(2,1)} %bitcast.79), calls=%async_computation.1 | async-start | bytes 8388608 | tf_op jit(solution)/shard_map/all_to_all | solution.py:112
  302.9 3.1 copy-start.4
  302.9 3.5 copy-start.9
  307.5 1.0 copy-start.5
  397.3 5.8 %copy-start.2 = (bf16[8,256,4,128]{3,2,1,0:T(4,128)(2,1)S(1)}, bf16[8,256,4,128]{3,2,1,0:T(4,128)(2,1)}, u32[]{:S(2)}) copy-start(bf16[8,256,4,128]{3,2,1,0:T(4,128)(2,1)} %copy-done.1) | copy-start | bytes 6291460
  397.3 102.3 %all-to-all-start = ((bf16[32,1,128,512]{3,2,1,0:T(8,128)(2,1)}), bf16[32,1,128,512]{3,2,1,0:T(8,128)(2,1)}, u32[]{:S(2)}, u32[]{:S(2)}) async-start(bf16[32,1,128,512]{3,2,1,0:T(8,128)(2,1)} %bitcast.78), calls=%async_computation | async-start | bytes 8388608 | tf_op jit(solution)/shard_map/all_to_all | solution.py:111
  499.6 4.7 copy-start
Sparse Core Ops, SparseCore 0:
  9.9 54.4 all-gather.5
  66.9 99.4 all-gather.3
  169.0 95.5 all-gather.7
where the time goes:
time: 514 us; the launch traced here: 513 us
  waiting for transfers between devices  404 us (79%)
  local copies, waits for them, and re-layouts  57.5 us (11%)
  matrix products  20 us (4%)
  between operations  14 us (3%)
  starting transfers between devices  11.7 us (2%)
  other arithmetic  5.99 us (1%)
    all_gather x1, waiting for transfers between devices, on_device(): lax.all_gather(values, 'seq', axis=0, tiled=True)  94.1 us
    all_gather x1, waiting for transfers between devices, on_device(): lax.all_gather(keys, 'seq', axis=0, tiled=True)  91.7 us
    all_to_all x1, waiting for transfers between devices, on_device(): lax.all_to_all(key_back, 'seq', split_axis=0, concat_axis=0, tiled=True)  87 us
    all_to_all x1, waiting for transfers between devices, on_device(): lax.all_to_all(value_back, 'seq', split_axis=0, concat_axis=0, tiled=True)  75.5 us
    all_gather x1, waiting for transfers between devices, on_device(): lax.all_gather(out_grad, 'mp', axis=1, tiled=True)  53.3 us
    unnamed x24, local copies, waits for them, and re-layouts  15.3 us
    dot_general x1, matrix products, on_device(): lax.dot_general(lax.all_gather(out_grad, 'mp', axis=1, tiled=True), out_w...  10.3 us
  transfers between devices with their start and end apart: 5, of which 5 were waited for; matrix products, arithmetic and copies ran while one was open for 9% of the time, Pallas kernels for 0%

commit v1 on v0

--- a/solution.py
+++ b/solution.py
@@ -7,6 +7,34 @@
 HEAD = 128
 BLOCK = 64
 NEIGH = 2
+
+
+def put_ports_up(local_array, at_axis):
+    local_array = jnp.moveaxis(local_array, 0, at_axis)
+    s_next = local_array.shape
+    return local_array.reshape(
+        *s_next[:at_axis], s_next[at_axis] * s_next[at_axis + 1], *s_next[at_axis + 2 :]
+    )
+
+
+def advance_joints_over_axis(u_in, axis_key, array_axis=1):
+    axis_n = lax.psum(1, axis_key)
+    leaves = [(tick, (tick + 1) % axis_n) for tick in range(axis_n)]
+    gallery = [(dev, no) for no, dev in leaves]
+    now, w2 = ([], [])
+    for nth in range(axis_n - 1):
+        if nth % 2 == 0:
+            later = lax.ppermute(now[-1] if now else u_in, axis_key, leaves)
+            now.append(later)
+        else:
+            q_next = lax.ppermute(w2[-1] if w2 else u_in, axis_key, gallery)
+            w2.append(q_next)
+    vec_out = jnp.stack([*now[::-1], u_in, *w2])
+    carry_out = lax.axis_index(axis_key)
+    r_now = len(now)
+    t_next = carry_out - r_now
+    vec_out = vec_out[(jnp.arange(axis_n) - t_next) % axis_n]
+    return put_ports_up(vec_out, array_axis)
 
 
 def rank_slots(owners):
@@ -28,7 +56,7 @@
     slot_cap = (slot_count + seq_count - 1) // seq_count
     score_scale = 1.0 / math.sqrt(HEAD)
     grad_out = lax.dot_general(
-        lax.all_gather(out_grad, "mp", axis=1, tiled=True),
+        advance_joints_over_axis(out_grad, "mp"),
         out_weight,
         (((1,), (1,)), ((), ())),
         preferred_element_type=jnp.float32,

time: 514 us -> 460 us (0.89)
  waiting for transfers between devices: 404 us -> 309 us
  local copies, waits for them, and re-layouts: 57.5 us -> 92.1 us
  starting transfers between devices: 11.7 us -> 16.9 us
    all_gather x1, waiting for transfers between devices: 91.7 us -> 1.48 us  [on_device(): lax.all_gather(keys, 'seq', axis=0, tiled=True)]
    all_gather x1 -> x0, waiting for transfers between devices: 53.3 us -> none  [on_device(): lax.all_gather(out_grad, 'mp', axis=1, tiled=True)]
    ppermute x0 -> x7, waiting for transfers between devices: none -> 49.3 us  [the longest x4 49.3 us: advance_joints_over_axis(): later = lax.ppermute(now[-1] if now else u_in, axis_key, leaves)]
    unnamed x24 -> x29, local copies, waits for them, and re-layouts: 15.3 us -> 27.8 us
    transpose x0 -> x1, local copies, waits for them, and re-layouts: none -> 11.5 us  [put_ports_up(): local_array = jnp.moveaxis(local_array, 0, at_axis)]
    gather x0 -> x1, local copies, waits for them, and re-layouts: none -> 8.19 us  [advance_joints_over_axis(): vec_out = vec_out[(jnp.arange(axis_n) - t_next) % axis_n]]
    ppermute x0 -> x7, starting transfers between devices: none -> 5.26 us  [the longest x3 5.24 us: advance_joints_over_axis(): q_next = lax.ppermute(w2[-1] if w2 else u_in, axis_key, gallery)]
  transfers between devices with their start and end apart: 5 -> 11, of which waited for: 5 -> 8; matrix products, arithmetic and copies ran while one was open for 9% -> 18% of each run, Pallas kernels for 0% -> 0%
where the time goes in v1:
time: 460 us; the launch traced here: 459 us
  waiting for transfers between devices  309 us (67%)
  local copies, waits for them, and re-layouts  92.1 us (20%)
  matrix products  20.2 us (4%)
  starting transfers between devices  16.9 us (4%)
  between operations  14.3 us (3%)
  other arithmetic  6.68 us (1%)
    all_gather x1, waiting for transfers between devices, on_device(): lax.all_gather(values, 'seq', axis=0, tiled=True)  94.1 us
    all_to_all x1, waiting for transfers between devices, on_device(): lax.all_to_all(key_back, 'seq', split_axis=0, concat_axis=0, tiled=True)  86.9 us
    all_to_all x1, waiting for transfers between devices, on_device(): lax.all_to_all(value_back, 'seq', split_axis=0, concat_axis=0, tiled=True)  75.4 us
    ppermute x4, waiting for transfers between devices, advance_joints_over_axis(): later = lax.ppermute(now[-1] if now else u_in, axis_key, leaves)  49.3 us
    unnamed x29, local copies, waits for them, and re-layouts  27.8 us
    transpose x1, local copies, waits for them, and re-layouts, put_ports_up(): local_array = jnp.moveaxis(local_array, 0, at_axis)  11.5 us
    dot_general x1, matrix products, on_device(): lax.dot_general(advance_joints_over_axis(out_grad, 'mp'), out_weight, (((...  10.5 us
  transfers between devices with their start and end apart: 11, of which 8 were waited for; matrix products, arithmetic and copies ran while one was open for 18% of the time, Pallas kernels for 0%

profile of v1, /device:TPU:2, one launch (start us, length us, event | category | flops | bytes accessed | tf_op | source)
XLA Modules:
  0.0 458.8 jit_solution(9793011754535120685)
XLA Ops:
  8.7 14.4 %collective-permute-done = bf16[512,1024]{1,0:T(8,128)(2,1)S(1)} collective-permute-done((bf16[512,1024]{1,0:T(8,128)(2,1)}, bf16[512,1024]{1,0:T(8,128)(2,1)S(1)}, u32[]{:S(2)}, u32[]{:S(2)}) %collective-permute-start) | collective-permute-done | bytes 1048608 | tf_op jit(solution)/shard_map/ppermute | solution.py:27
  23.1 1.7 collective-permute-start.4
  24.8 12.6 %collective-permute-done.1 = bf16[512,1024]{1,0:T(8,128)(2,1)} collective-permute-done((bf16[512,1024]{1,0:T(8,128)(2,1)S(1)}, bf16[512,1024]{1,0:T(8,128)(2,1)}, u32[]{:S(2)}, u32[]{:S(2)}) %collective-permute-start.1) | collective-permute-done | bytes 1048608 | tf_op jit(solution)/shard_map/ppermute | solution.py:27
  38.6 1.8 collective-permute-start.5
  40.3 11.6 %collective-permute-done.2 = bf16[512,1024]{1,0:T(8,128)(2,1)} collective-permute-done((bf16[512,1024]{1,0:T(8,128)(2,1)}, bf16[512,1024]{1,0:T(8,128)(2,1)}, u32[]{:S(2)}, u32[]{:S(2)}) %collective-permute-start.2) | collective-permute-done | bytes 1048608 | tf_op jit(solution)/shard_map/ppermute | solution.py:27
  52.0 1.2 reshape.496
  54.1 1.7 collective-permute-start.6
  55.9 10.6 %collective-permute-done.3 = bf16[512,1024]{1,0:T(8,128)(2,1)} collective-permute-done((bf16[512,1024]{1,0:T(8,128)(2,1)}, bf16[512,1024]{1,0:T(8,128)(2,1)}, u32[]{:S(2)}, u32[]{:S(2)}) %collective-permute-start.3) | collective-permute-done | bytes 1048608 | tf_op jit(solution)/shard_map/ppermute | solution.py:27
  66.5 2.3 bitcast_dynamic-update-slice_fusion.7
  68.8 2.3 bitcast_dynamic-update-slice_fusion.6
  71.1 2.4 bitcast_dynamic-update-slice_fusion.5
  73.5 1.1 bitcast_dynamic-update-slice_fusion.4
  74.6 1.0 bitcast_dynamic-update-slice_fusion.3
  75.6 1.1 bitcast_dynamic-update-slice_fusion.2
  76.7 2.3 bitcast_dynamic-update-slice_fusion.1
  79.0 1.1 bitcast_dynamic-update-slice_fusion
  80.1 8.2 %gather_fusion = bf16[8,512,1024]{2,1,0:T(8,128)(2,1)} fusion(bf16[8,512,1024]{2,1,0:T(8,128)(2,1)} %bitcast_dynamic-update-slice_fusion, s32[1024]{0:T(1024)S(1)} %pad_clamp_fusion), kind=kCustom, calls=%fused_computation.2 | custom fusion | bytes 16777248 | tf_op jit(solution)/shard_map/gather | solution.py:36
  88.3 11.5 %copy.99 = bf16[512,8,1024]{0,2,1:T(8,128)(2,1)} copy(bf16[512,8,1024]{2,0,1:T(8,128)(2,1)} %bitcast.98) | data formatting | bytes 16777216 | tf_op jit(solution)/shard_map/transpose | solution.py:13
  99.8 10.5 %convolution_convert_fusion.2 = bf16[512,512]{1,0:T(8,128)(2,1)S(1)} fusion(bf16[512,8192]{0,1:T(8,128)(2,1)} %bitcast.103, bf16[512,8192]{1,0:T(8,128)(2,1)} %param.10), kind=kOutput, calls=%fused_computation.31 | convolution fusion | flops 4295229440 | bytes 17301504 | tf_op jit(solution)/shard_map/dot_general | solution.py:58
  110.4 1.5 all-gather.3.cloned.1.call-done
  111.9 4.1 gather_fusion.1
  116.0 94.1 %all-gather.5.cloned.1.call-done = bf16[64,128,512]{2,1,0:T(8,128)(2,1)} async-done(((bf16[2,128,512]{2,1,0:T(8,128)(2,1)}), bf16[64,128,512]{2,1,0:T(8,128)(2,1)}) %all-gather.5.cloned.1.call-update) | async-done | bytes 8388624 | tf_op jit(solution)/shard_map/all_gather | solution.py:78
  210.1 5.4 %gather_fusion.2 = bf16[16,128,512]{2,1,0:T(8,128)(2,1)} fusion(bf16[64,128,512]{2,1,0:T(8,128)(2,1)} %all-gather.5.cloned.1.call-done, s32[1024]{0:T(1024)S(1)} %pad_clamp_fusion.1), kind=kCustom, calls=%fused_computation.1.clone | custom fusion | bytes 4194368 | tf_op jit(solution)/shard_map/jit(_take)/gather | solution.py:81
  215.5 4.0 broadcast_select_fusion.1
  219.5 2.5 reshape.495
  223.4 1.7 bitcast_reduce_fusion
  225.2 1.3 copy-done.7
  226.5 0.9 convert_bitcast_fusion
  227.4 2.5 copy.124
  229.9 2.7 reshape.557
  232.7 2.4 broadcast.416.clone
  235.1 5.3 %scatter_fusion.1 = bf16[32,128,512]{2,1,0:T(8,128)(2,1)} fusion(bf16[32,128,512]{2,1,0:T(8,128)(2,1)} %broadcast.416.clone, s32[16]{0:T(128)S(1)} %fusion.55, bf16[16,128,512]{2,1,0:T(8,128)(2,1)S(1)} %reshape.557), kind=kCustom, calls=%fused_computation.4 | custom fusion | bytes 6291520 | tf_op jit(solution)/shard_map/scatter | solution.py:135
  240.4 6.0 %all-to-all-start.1 = ((bf16[32,1,128,512]{3,2,1,0:T(8,128)(2,1)}), bf16[32,1,128,512]{3,2,1,0:T(8,128)(2,1)}, u32[]{:S(2)}, u32[]{:S(2)}) async-start(bf16[32,1,128,512]{3,2,1,0:T(8,128)(2,1)} %bitcast.100), calls=%async_computation.1 | async-start | bytes 8388608 | tf_op jit(solution)/shard_map/all_to_all | solution.py:140
  246.4 2.1 reshape.499
  248.5 3.1 fusion.28
  252.0 1.0 multiply_convert_fusion.1
  254.0 3.0 copy.123
  257.0 2.7 reshape.556
  259.7 2.4 broadcast.416.clone.1
  262.2 5.2 %scatter_fusion = bf16[32,128,512]{2,1,0:T(8,128)(2,1)} fusion(bf16[32,128,512]{2,1,0:T(8,128)(2,1)} %broadcast.416.clone.1, s32[16]{0:T(128)S(1)} %fusion.55, bf16[16,128,512]{2,1,0:T(8,128)(2,1)S(1)} %reshape.556), kind=kCustom, calls=%fused_computation.3 | custom fusion | bytes 6291520 | tf_op jit(solution)/shard_map/scatter | solution.py:129
  267.4 75.4 %all-to-all-done.1 = bf16[32,1,128,512]{3,2,1,0:T(8,128)(2,1)} async-done(((bf16[32,1,128,512]{3,2,1,0:T(8,128)(2,1)}), bf16[32,1,128,512]{3,2,1,0:T(8,128)(2,1)}, u32[]{:S(2)}, u32[]{:S(2)}) %all-to-all-start.1) | async-done | bytes 4194336 | tf_op jit(solution)/shard_map/all_to_all | solution.py:140
  342.8 5.5 %all-to-all-start = ((bf16[32,1,128,512]{3,2,1,0:T(8,128)(2,1)}), bf16[32,1,128,512]{3,2,1,0:T(8,128)(2,1)}, u32[]{:S(2)}, u32[]{:S(2)}) async-start(bf16[32,1,128,512]{3,2,1,0:T(8,128)(2,1)} %bitcast.99), calls=%async_computation | async-start | bytes 8388608 | tf_op jit(solution)/shard_map/all_to_all | solution.py:139
  348.6 1.7 fusion.31
  350.7 0.9 copy.166
  351.6 6.5 %copy.130 = bf16[4,8,128,512]{3,1,2,0:T(8,128)(2,1)} copy(bf16[4,8,128,512]{3,2,1,0:T(8,128)(2,1)} %bitcast.38) | data formatting | bytes 8388608
  358.1 86.9 %all-to-all-done = bf16[32,1,128,512]{3,2,1,0:T(8,128)(2,1)} async-done(((bf16[32,1,128,512]{3,2,1,0:T(8,128)(2,1)}), bf16[32,1,128,512]{3,2,1,0:T(8,128)(2,1)}, u32[]{:S(2)}, u32[]{:S(2)}) %all-to-all-start) | async-done | bytes 4194336 | tf_op jit(solution)/shard_map/all_to_all | solution.py:139
  445.0 4.7 %copy.128 = bf16[4,8,128,512]{3,1,2,0:T(8,128)(2,1)S(1)} copy(bf16[4,8,128,512]{3,2,1,0:T(8,128)(2,1)} %bitcast.33) | data formatting | bytes 8388608
  451.1 0.8 copy_bitcast_fusion.1
  (52 shorter events, 8.4 us)
Async XLA Ops:
  7.2 104.8 %all-gather.3.cloned.1.call-start = ((), (), s32[]{:S(2)}) async-start(), calls=%async_computation.2 | async-start | bytes 8650752 | tf_op jit(solution)/shard_map/all_gather | solution.py:77
  7.9 202.2 %all-gather.5.cloned.1.call-start = ((), (), s32[]{:S(2)}) async-start(), calls=%async_computation.3 | async-start | bytes 8650752 | tf_op jit(solution)/shard_map/all_gather | solution.py:78
  8.6 14.4 %collective-permute-start = (bf16[512,1024]{1,0:T(8,128)(2,1)}, bf16[512,1024]{1,0:T(8,128)(2,1)S(1)}, u32[]{:S(2)}, u32[]{:S(2)}) collective-permute-start(bf16[512,1024]{1,0:T(8,128)(2,1)} %param.9), channel_id=1, source_target_pairs={{0,1},{1,2},{2,3},{3,4},{4,5},{5,6},{6,7},{7,0},{8,9},{9,10},{10,1... | collective-permute-start | bytes 3145736 | tf_op jit(solution)/shard_map/ppermute | solution.py:27
  23.1 14.3 %collective-permute-start.1 = (bf16[512,1024]{1,0:T(8,128)(2,1)S(1)}, bf16[512,1024]{1,0:T(8,128)(2,1)}, u32[]{:S(2)}, u32[]{:S(2)}) collective-permute-start(bf16[512,1024]{1,0:T(8,128)(2,1)S(1)} %collective-permute-done), channel_id=1, source_target_pairs={{0,1},{1,2},{2,3},{3,4},{4,5},{5,6},{6,7},{7,0},{8,9},{9,10},{10,1... | collective-permute-start | bytes 3145736 | tf_op jit(solution)/shard_map/ppermute | solution.py:27
  23.1 15.5 %collective-permute-start.4 = (bf16[512,1024]{1,0:T(8,128)(2,1)}, bf16[512,1024]{1,0:T(8,128)(2,1)S(1)}, u32[]{:S(2)}, u32[]{:S(2)}) collective-permute-start(bf16[512,1024]{1,0:T(8,128)(2,1)} %param.9), channel_id=1, source_target_pairs={{1,0},{2,1},{3,2},{4,3},{5,4},{6,5},{7,6},{0,7},{9,8},{10,9},{11,1... | collective-permute-start | bytes 3145736 | tf_op jit(solution)/shard_map/ppermute | solution.py:30
  37.4 14.5 %collective-permute-start.2 = (bf16[512,1024]{1,0:T(8,128)(2,1)}, bf16[512,1024]{1,0:T(8,128)(2,1)}, u32[]{:S(2)}, u32[]{:S(2)}) collective-permute-start(bf16[512,1024]{1,0:T(8,128)(2,1)} %collective-permute-done.1), channel_id=1, source_target_pairs={{0,1},{1,2},{2,3},{3,4},{4,5},{5,6},{6,7},{7,0},{8,9},{9,10},{10,1... | collective-permute-start | bytes 3145736 | tf_op jit(solution)/shard_map/ppermute | solution.py:27
  38.6 15.6 %collective-permute-start.5 = (bf16[512,1024]{1,0:T(8,128)(2,1)S(1)}, bf16[512,1024]{1,0:T(8,128)(2,1)}, u32[]{:S(2)}, u32[]{:S(2)}) collective-permute-start(bf16[512,1024]{1,0:T(8,128)(2,1)S(1)} %collective-permute-done.4), channel_id=1, source_target_pairs={{1,0},{2,1},{3,2},{4,3},{5,4},{6,5},{7,6},{0,7},{9,8},{10,9},{11,1... | collective-permute-start | bytes 3145736 | tf_op jit(solution)/shard_map/ppermute | solution.py:30
  52.0 14.5 %collective-permute-start.3 = (bf16[512,1024]{1,0:T(8,128)(2,1)}, bf16[512,1024]{1,0:T(8,128)(2,1)}, u32[]{:S(2)}, u32[]{:S(2)}) collective-permute-start(bf16[512,1024]{1,0:T(8,128)(2,1)} %collective-permute-done.2), channel_id=1, source_target_pairs={{0,1},{1,2},{2,3},{3,4},{4,5},{5,6},{6,7},{7,0},{8,9},{9,10},{10,1... | collective-permute-start | bytes 3145736 | tf_op jit(solution)/shard_map/ppermute | solution.py:27
  54.1 24.9 %collective-permute-start.6 = (bf16[512,1024]{1,0:T(8,128)(2,1)}, bf16[512,1024]{1,0:T(8,128)(2,1)S(1)}, u32[]{:S(2)}, u32[]{:S(2)}) collective-permute-start(bf16[512,1024]{1,0:T(8,128)(2,1)} %collective-permute-done.5), channel_id=1, source_target_pairs={{1,0},{2,1},{3,2},{4,3},{5,4},{6,5},{7,6},{0,7},{9,8},{10,9},{11,1... | collective-permute-start | bytes 3145736 | tf_op jit(solution)/shard_map/ppermute | solution.py:30
  71.1 3.5 copy-start.6
  222.1 1.4 copy-start.1
  225.2 1.3 copy-start.7
  240.4 6.0 %copy-start.3 = (bf16[16,128,512]{2,1,0:T(8,128)(2,1)S(1)}, bf16[16,128,512]{2,1,0:T(8,128)(2,1)}, u32[]{:S(2)}) copy-start(bf16[16,128,512]{2,1,0:T(8,128)(2,1)} %get-tuple-element.9) | copy-start | bytes 6291460
  240.4 102.4 %all-to-all-start.1 = ((bf16[32,1,128,512]{3,2,1,0:T(8,128)(2,1)}), bf16[32,1,128,512]{3,2,1,0:T(8,128)(2,1)}, u32[]{:S(2)}, u32[]{:S(2)}) async-start(bf16[32,1,128,512]{3,2,1,0:T(8,128)(2,1)} %bitcast.100), calls=%async_computation.1 | async-start | bytes 8388608 | tf_op jit(solution)/shard_map/all_to_all | solution.py:140
  248.5 3.1 copy-start.4
  248.5 3.5 copy-start.8
  253.0 1.0 copy-start.5
  342.8 5.8 %copy-start.2 = (bf16[8,256,4,128]{3,2,1,0:T(4,128)(2,1)S(1)}, bf16[8,256,4,128]{3,2,1,0:T(4,128)(2,1)}, u32[]{:S(2)}) copy-start(bf16[8,256,4,128]{3,2,1,0:T(4,128)(2,1)} %copy-done.1) | copy-start | bytes 6291460
  342.8 102.2 %all-to-all-start = ((bf16[32,1,128,512]{3,2,1,0:T(8,128)(2,1)}), bf16[32,1,128,512]{3,2,1,0:T(8,128)(2,1)}, u32[]{:S(2)}, u32[]{:S(2)}) async-start(bf16[32,1,128,512]{3,2,1,0:T(8,128)(2,1)} %bitcast.99), calls=%async_computation | async-start | bytes 8388608 | tf_op jit(solution)/shard_map/all_to_all | solution.py:139
  445.0 4.7 %copy-start = (bf16[4,8,128,512]{3,1,2,0:T(8,128)(2,1)S(1)}, bf16[4,8,128,512]{3,1,2,0:T(8,128)(2,1)}, u32[]{:S(2)}) copy-start(bf16[4,8,128,512]{3,1,2,0:T(8,128)(2,1)} %copy.130) | copy-start | bytes 12582916
Sparse Core Ops, SparseCore 0:
  10.6 101.2 all-gather.2
  114.5 95.5 all-gather.4
